TPU v7x, 32 devices: a whole 2x2x4 slice. The times are simulated.
32 devices in a mesh: dp: 8 (over z, x), tensor: 4 (over y, core).
Axes of the slice: x: 2, y: 2, z: 4, core: 2. Of those that a mesh axis runs over, the one named last changes fastest.
Arguments:
- inputs: bfloat16 [2048, 2048], P('dp'), may hold values from -6 to 6
- document: int32 [2048], P('dp'), may hold values from 0 to 8, as said below
- query_weight: bfloat16 [2048, 2048], P(None, 'tensor'), may hold values from -0.125 to 0.125
- key_weight: bfloat16 [2048, 2048], P(None, 'tensor'), may hold values from -0.125 to 0.125
- value_weight: bfloat16 [2048, 3456], P(None, 'tensor'), may hold values from -0.125 to 0.125
- gate_weight: bfloat16 [2048, 3456], P(None, 'tensor'), may hold values from -0.125 to 0.125
- out_weight: bfloat16 [3456, 2048], P('tensor'), may hold values from -0.109375 to 0.109375
- inner_weight: bfloat16 [2048, 3456], P(None, 'tensor'), may hold values from -0.125 to 0.125
- linear_weight: bfloat16 [2048, 3456], P(None, 'tensor'), may hold values from -0.125 to 0.125
- down_weight: bfloat16 [3456, 2048], P('tensor'), may hold values from -0.109375 to 0.109375
- first_gain: float32 [2048], replicated, may hold values from 0.5 to 1.5
- first_bias: float32 [2048], replicated, may hold values from -3 to 3
- head_gain: float32 [3456], P('tensor'), may hold values from 0.5 to 1.5
- second_gain: float32 [2048], replicated, may hold values from 0.5 to 1.5
- second_bias: float32 [2048], replicated, may hold values from -3 to 3
- cotangent: bfloat16 [2048, 2048], P('dp'), may hold values from -8 to 8
Outputs:
- outputs: float32 [2048, 2048], P('dp')
- grad_inputs: float32 [2048, 2048], P('dp')
- grad_query: float32 [2048, 2048], P('dp', 'tensor')
- grad_key: float32 [2048, 2048], P('dp', 'tensor')
- grad_value: float32 [2048, 3456], P('dp', 'tensor')
- grad_gate: float32 [2048, 3456], P('dp', 'tensor')
- grad_out: float32 [3456, 2048], P('tensor', 'dp')
- grad_inner: float32 [2048, 3456], P('dp', 'tensor')
- grad_linear: float32 [2048, 3456], P('dp', 'tensor')
- grad_down: float32 [3456, 2048], P('tensor', 'dp')
- grad_first_gain: float32 [2048], replicated
- grad_first_bias: float32 [2048], replicated
- grad_head_gain: float32 [3456], P('tensor')
- grad_second_gain: float32 [2048], replicated
- grad_second_bias: float32 [2048], replicated
Inputs may be any that keep to these rules, and one draw needn't show every extreme that they name: `document`: within each dp block of 256 slots the sequence numbers never fall; the live slots come first and hold numbers below 8, the last live one 8 - 1; the other slots hold 8. One block is all live and another has exactly 128 live slots.
All inputs are finite; a program needn't handle non-finite values.
Results may differ from a plain program's by a relative error of at most 0.015.
Values sent between devices are 32-bit elements; how exact they have to be, the bound alone decides.
No kernel may reach another device: no remote copies, remote signals or barrier semaphores. Data moves between devices by JAX's collectives and lax.ppermute only.
A program may use at most 192 MiB of HBM per device.

v0:
```python
import jax
import jax.numpy as jnp
from jax import lax
from jax.sharding import PartitionSpec as P

KD = 256
VD = 432
DOCS_DEV = 8


EPS = 1e-05
HEAD_EPS = 0.25


def norm_rows(value, gain, bias, epsilon):
    center = value - jnp.mean(value, -1, keepdims=True)
    inverse = lax.rsqrt(jnp.mean(center * center, -1, keepdims=True) + epsilon)
    unit = center * inverse
    return (unit * gain + bias, unit, inverse)


def norm_back(upstream, unit, inverse, gain):
    scaled = upstream * gain
    result = inverse * (
        scaled
        - jnp.mean(scaled, -1, keepdims=True)
        - unit * jnp.mean(scaled * unit, -1, keepdims=True)
    )
    return (result, jnp.sum(upstream * unit, 0), jnp.sum(upstream, 0))


def decay_table(document, first_head, head_count):
    heads = (first_head + jnp.arange(head_count)).astype(jnp.float32)
    log_rate = jnp.log1p(-jnp.exp2(-5.0 - heads))
    places = jnp.arange(document.shape[0])
    spread = (places[:, None] - places[None, :]).astype(jnp.float32)
    allowed = (places[:, None] >= places[None, :]) & (document[:, None] == document[None, :])
    safe = jnp.where(allowed, spread, 0.0)
    return jnp.where(allowed[None], jnp.exp(safe[None] * log_rate[:, None, None]), 0.0)


def body(
    inputs,
    document,
    query_weight,
    key_weight,
    value_weight,
    gate_weight,
    out_weight,
    inner_weight,
    linear_weight,
    down_weight,
    first_gain,
    first_bias,
    head_gain,
    second_gain,
    second_bias,
    cotangent,
):
    f32 = jnp.float32
    bf16 = jnp.bfloat16
    residual_in = inputs.astype(f32)
    rows = inputs.shape[0]
    head_count = query_weight.shape[1] // KD
    local_values = value_weight.shape[1]
    first_norm, first_hat, first_inv = norm_rows(residual_in, first_gain, first_bias, EPS)
    normed_one = first_norm.astype(bf16)
    queries = jnp.dot(normed_one, query_weight, preferred_element_type=f32)
    keys_raw = jnp.dot(normed_one, key_weight, preferred_element_type=f32)
    values_raw = jnp.dot(normed_one, value_weight, preferred_element_type=f32)
    gates_raw = jnp.dot(normed_one, gate_weight, preferred_element_type=f32)
    query_bf = queries.astype(bf16).reshape(rows, head_count, KD)
    key_bf = (keys_raw * KD ** (-0.5)).astype(bf16).reshape(rows, head_count, KD)
    value_bf = values_raw.astype(bf16).reshape(rows, head_count, VD)
    decay = decay_table(document, lax.axis_index("tensor") * head_count, head_count)
    scores = jnp.einsum("nhk,mhk->hnm", query_bf, key_bf, preferred_element_type=f32) * decay
    score_bf = scores.astype(bf16)
    mixed = jnp.einsum("hnm,mhv->nhv", score_bf, value_bf, preferred_element_type=f32)
    gain_heads = head_gain.reshape(head_count, VD)
    normed_heads, head_hat, head_inv = norm_rows(mixed, gain_heads, 0.0, HEAD_EPS)
    normed_flat = normed_heads.reshape(rows, local_values)
    sigma = jax.nn.sigmoid(gates_raw)
    swish = gates_raw * sigma
    gated = (swish * normed_flat).astype(bf16)
    branch = lax.psum(jnp.dot(gated, out_weight, preferred_element_type=f32), "tensor")
    middle = residual_in + branch
    second_norm, second_hat, second_inv = norm_rows(middle, second_gain, second_bias, EPS)
    normed_two = second_norm.astype(bf16)
    inner = jnp.dot(normed_two, inner_weight, preferred_element_type=f32)
    linear = jnp.dot(normed_two, linear_weight, preferred_element_type=f32)
    cumulative = 0.5 * (1.0 + jax.scipy.special.erf(inner * 0.7071067811865476))
    gelu_inner = inner * cumulative
    hidden = (gelu_inner * linear).astype(bf16)
    feedforward = lax.psum(jnp.dot(hidden, down_weight, preferred_element_type=f32), "tensor")
    outputs = middle + feedforward
    live = (document < DOCS_DEV).astype(f32)
    grad_top = cotangent.astype(f32) * live[:, None]
    grad_top_bf = grad_top.astype(bf16)
    grad_down = jnp.dot(hidden.T, grad_top_bf, preferred_element_type=f32)
    grad_hidden = jnp.dot(grad_top_bf, down_weight.T, preferred_element_type=f32)
    slope = cumulative + inner * jnp.exp(-0.5 * inner * inner) * 0.3989422804014327
    grad_inner_bf = (grad_hidden * linear * slope).astype(bf16)
    grad_linear_bf = (grad_hidden * gelu_inner).astype(bf16)
    grad_inner = jnp.dot(normed_two.T, grad_inner_bf, preferred_element_type=f32)
    grad_linear = jnp.dot(normed_two.T, grad_linear_bf, preferred_element_type=f32)
    local_two = jnp.dot(grad_inner_bf, inner_weight.T, preferred_element_type=f32) + jnp.dot(
        grad_linear_bf, linear_weight.T, preferred_element_type=f32
    )
    grad_normed_two = lax.psum(local_two, "tensor")
    part_two, grad_second_gain, grad_second_bias = norm_back(
        grad_normed_two, second_hat, second_inv, second_gain
    )
    grad_middle = grad_top + part_two
    grad_middle_bf = grad_middle.astype(bf16)
    grad_out = jnp.dot(gated.T, grad_middle_bf, preferred_element_type=f32)
    grad_gated = jnp.dot(grad_middle_bf, out_weight.T, preferred_element_type=f32)
    grad_gates_bf = (grad_gated * normed_flat * sigma * (1.0 + gates_raw * (1.0 - sigma))).astype(
        bf16
    )
    grad_normed = (grad_gated * swish).reshape(rows, head_count, VD)
    grad_mixed, grad_gain_heads, unused_bias = norm_back(
        grad_normed, head_hat, head_inv, gain_heads
    )
    grad_mixed_bf = grad_mixed.astype(bf16)
    grad_scores = jnp.einsum("nhv,mhv->hnm", grad_mixed_bf, value_bf, preferred_element_type=f32)
    grad_values = jnp.einsum("hnm,nhv->mhv", score_bf, grad_mixed_bf, preferred_element_type=f32)
    grad_masked = (grad_scores * decay).astype(bf16)
    grad_queries = jnp.einsum("hnm,mhk->nhk", grad_masked, key_bf, preferred_element_type=f32)
    grad_keys = jnp.einsum(
        "hnm,nhk->mhk", grad_masked, query_bf, preferred_element_type=f32
    ) * KD ** (-0.5)
    grad_queries_bf = grad_queries.astype(bf16).reshape(rows, head_count * KD)
    grad_keys_bf = grad_keys.astype(bf16).reshape(rows, head_count * KD)
    grad_values_bf = grad_values.astype(bf16).reshape(rows, local_values)
    grad_query = jnp.dot(normed_one.T, grad_queries_bf, preferred_element_type=f32)
    grad_key = jnp.dot(normed_one.T, grad_keys_bf, preferred_element_type=f32)
    grad_value = jnp.dot(normed_one.T, grad_values_bf, preferred_element_type=f32)
    grad_gate = jnp.dot(normed_one.T, grad_gates_bf, preferred_element_type=f32)
    local_one = (
        jnp.dot(grad_queries_bf, query_weight.T, preferred_element_type=f32)
        + jnp.dot(grad_keys_bf, key_weight.T, preferred_element_type=f32)
        + jnp.dot(grad_values_bf, value_weight.T, preferred_element_type=f32)
        + jnp.dot(grad_gates_bf, gate_weight.T, preferred_element_type=f32)
    )
    grad_normed_one = lax.psum(local_one, "tensor")
    part_one, grad_first_gain, grad_first_bias = norm_back(
        grad_normed_one, first_hat, first_inv, first_gain
    )
    grad_inputs = grad_middle + part_one
    (
        summed_query,
        summed_key,
        summed_value,
        summed_gate,
        summed_out,
        summed_inner,
        summed_linear,
        summed_down,
    ) = (
        lax.psum_scatter(grad_query, "dp", scatter_dimension=0, tiled=True),
        lax.psum_scatter(grad_key, "dp", scatter_dimension=0, tiled=True),
        lax.psum_scatter(grad_value, "dp", scatter_dimension=0, tiled=True),
        lax.psum_scatter(grad_gate, "dp", scatter_dimension=0, tiled=True),
        lax.psum_scatter(grad_out, "dp", scatter_dimension=1, tiled=True),
        lax.psum_scatter(grad_inner, "dp", scatter_dimension=0, tiled=True),
        lax.psum_scatter(grad_linear, "dp", scatter_dimension=0, tiled=True),
        lax.psum_scatter(grad_down, "dp", scatter_dimension=1, tiled=True),
    )
    first_gain_sum, first_bias_sum, head_gain_sum, second_gain_sum, second_bias_sum = lax.psum(
        (
            grad_first_gain,
            grad_first_bias,
            grad_gain_heads.reshape(local_values),
            grad_second_gain,
            grad_second_bias,
        ),
        "dp",
    )
    return (
        outputs,
        grad_inputs,
        summed_query,
        summed_key,
        summed_value,
        summed_gate,
        summed_out,
        summed_inner,
        summed_linear,
        summed_down,
        first_gain_sum,
        first_bias_sum,
        head_gain_sum,
        second_gain_sum,
        second_bias_sum,
    )


def solution(mesh):
    in_specs = (
        P("dp", None),
        P("dp"),
        P(None, "tensor"),
        P(None, "tensor"),
        P(None, "tensor"),
        P(None, "tensor"),
        P("tensor", None),
        P(None, "tensor"),
        P(None, "tensor"),
        P("tensor", None),
        P(),
        P(),
        P("tensor"),
        P(),
        P(),
        P("dp", None),
    )
    out_specs = (
        P("dp", None),
        P("dp", None),
        P("dp", "tensor"),
        P("dp", "tensor"),
        P("dp", "tensor"),
        P("dp", "tensor"),
        P("tensor", "dp"),
        P("dp", "tensor"),
        P("dp", "tensor"),
        P("tensor", "dp"),
        P(),
        P(),
        P("tensor"),
        P(),
        P(),
    )
    return jax.shard_map(body, mesh=mesh, in_specs=in_specs, out_specs=out_specs, check_vma=False)
```

profile of v0, /device:TPU:0, one launch (start us, length us, event | category | flops | bytes accessed | tf_op | source)
XLA Modules:
  0.0 1252.0 jit_solution(17441703664151072953)
XLA Ops:
  23.2 3.6 convolution_convert_fusion.1
  31.9 4.9 fusion.27
  41.6 4.4 fusion.39
  46.0 48.4 %all-reduce.6.cloned.1.call-done = f32[256,2048]{1,0:T(8,128)} async-done(((f32[256,2048]{1,0:T(8,128)}), f32[256,2048]{1,0:T(8,128)}) %all-reduce.6.cloned.1.call-update) | async-done | bytes 2097168 | tf_op jit(solution)/shard_map/psum | solution.py:85
  107.4 4.9 fusion.44
  112.3 45.6 %all-reduce.8.cloned.1.call-done = f32[256,2048]{1,0:T(8,128)} async-done(((f32[256,2048]{1,0:T(8,128)}), f32[256,2048]{1,0:T(8,128)}) %all-reduce.8.cloned.1.call-update) | async-done | bytes 2097168 | tf_op jit(solution)/shard_map/psum | solution.py:109
  183.9 5.8 fusion.43
  190.0 5.9 fusion.37
  196.0 5.4 fusion.66
  201.5 5.8 fusion.33
  207.3 5.1 fusion.45
  212.5 5.1 fusion.47
  217.8 43.9 %all-reduce.10.cloned.1.call-done = (f32[256,2048]{1,0:T(8,128)}, f32[256,2048]{1,0:T(8,128)}) async-done(((f32[256,2048]{1,0:T(8,128)}, f32[256,2048]{1,0:T(8,128)}), (f32[256,2048]{1,0:T(8,128)}, f32[256,2048]{1,0:T(8,128)})) %all-reduce.10.cloned.1.call-update) | async-done | bytes 4194320 | tf_op jit(solution)/shard_map/psum | solution.py:94
  261.7 3.4 add.136
  266.7 40.5 %all-reduce = (f32[2048]{0:T(1024)}, f32[2048]{0:T(1024)}, f32[864]{0:T(1024)}, f32[2048]{0:T(1024)}, f32[2048]{0:T(1024)}) all-reduce(f32[2048]{0:T(1024)S(1)} %get-tuple-element.17, f32[2048]{0:T(1024)S(1)} %get-tuple-element.22, f32[864]{0:T(1024)S(1)} %reshape.226, ...), channel_id=1, replica_groups=mesh['dp'=8,'tensor'=4] {'dp'}, use_global_device_ids=true, to_apply=%region_25.26 | all-reduce | flops 9056 | bytes 72448 | tf_op jit(solution)/shard_map/psum | solution.py:169
  308.0 4.9 fusion.13
  313.0 42.2 %reduce-scatter.11.cloned.1.call-done = f32[256,512]{1,0:T(8,128)} async-done(((f32[2048,512]{1,0:T(8,128)}), f32[256,512]{1,0:T(8,128)}) %reduce-scatter.11.cloned.1.call-update) | async-done | bytes 524304 | tf_op jit(solution)/shard_map/reduce_scatter | solution.py:161
  355.2 92.1 %reduce-scatter.9.cloned.1.call-done = f32[256,512]{1,0:T(8,128)} async-done(((f32[2048,512]{1,0:T(8,128)}), f32[256,512]{1,0:T(8,128)}) %reduce-scatter.9.cloned.1.call-update) | async-done | bytes 524304 | tf_op jit(solution)/shard_map/reduce_scatter | solution.py:160
  447.2 133.4 %reduce-scatter.21.cloned.1.call-done = f32[256,864]{0,1:T(8,128)} async-done(((f32[2048,864]{0,1:T(8,128)}), f32[256,864]{0,1:T(8,128)}) %reduce-scatter.21.cloned.1.call-update) | async-done | bytes 884752 | tf_op jit(solution)/shard_map/reduce_scatter | solution.py:166
  580.6 133.0 %reduce-scatter.23.cloned.1.call-done = f32[864,256]{1,0:T(8,128)} async-done(((f32[864,2048]{1,0:T(8,128)}), f32[864,256]{1,0:T(8,128)}) %reduce-scatter.23.cloned.1.call-update) | async-done | bytes 884752 | tf_op jit(solution)/shard_map/reduce_scatter | solution.py:167
  713.6 133.0 %reduce-scatter.19.cloned.1.call-done = f32[256,864]{0,1:T(8,128)} async-done(((f32[2048,864]{0,1:T(8,128)}), f32[256,864]{0,1:T(8,128)}) %reduce-scatter.19.cloned.1.call-update) | async-done | bytes 884752 | tf_op jit(solution)/shard_map/reduce_scatter | solution.py:165
  846.6 133.0 %reduce-scatter.17.cloned.1.call-done = f32[864,256]{1,0:T(8,128)} async-done(((f32[864,2048]{1,0:T(8,128)}), f32[864,256]{1,0:T(8,128)}) %reduce-scatter.17.cloned.1.call-update) | async-done | bytes 884752 | tf_op jit(solution)/shard_map/reduce_scatter | solution.py:164
  979.6 132.9 %reduce-scatter.13.cloned.1.call-done = f32[256,864]{0,1:T(8,128)} async-done(((f32[2048,864]{0,1:T(8,128)}), f32[256,864]{0,1:T(8,128)}) %reduce-scatter.13.cloned.1.call-update) | async-done | bytes 884752 | tf_op jit(solution)/shard_map/reduce_scatter | solution.py:162
  1112.5 133.0 %reduce-scatter.15.cloned.1.call-done = f32[256,864]{0,1:T(8,128)} async-done(((f32[2048,864]{0,1:T(8,128)}), f32[256,864]{0,1:T(8,128)}) %reduce-scatter.15.cloned.1.call-update) | async-done | bytes 884752 | tf_op jit(solution)/shard_map/reduce_scatter | solution.py:163
  (213 shorter events, 67.2 us)
Async XLA Ops:
  7.2 93.3 %copy-start = (bf16[2048,864]{0,1:T(8,128)(2,1)S(1)}, bf16[2048,864]{0,1:T(8,128)(2,1)}, u32[]{:S(2)}) copy-start(bf16[2048,864]{0,1:T(8,128)(2,1)} %param.23) | copy-start | bytes 10616836
  7.2 5.9 copy-start.40
  7.2 5.9 copy-start.41
  7.2 87.2 %all-reduce.6.cloned.1.call-start = ((), (), s32[]{:S(2)}) async-start(), calls=%async_computation.8 | async-start | bytes 4194304 | tf_op jit(solution)/shard_map/psum | solution.py:85
  40.1 117.7 %all-reduce.8.cloned.1.call-start = ((), (), s32[]{:S(2)}) async-start(), calls=%async_computation.9 | async-start | bytes 4194304 | tf_op jit(solution)/shard_map/psum | solution.py:109
  106.2 51.6 %copy-start.5 = (f32[256,2048]{1,0:T(8,128)S(1)}, f32[256,2048]{1,0:T(8,128)}, u32[]{:S(2)}) copy-start(f32[256,2048]{1,0:T(8,128)} %copy-done.4) | copy-start | bytes 6291460
  106.3 51.6 %copy-start.53 = (f32[2048]{0:T(1024)S(1)}, f32[2048]{0:T(1024)}, u32[]{:S(2)}) copy-start(f32[2048]{0:T(1024)} %param.29) | copy-start | bytes 24580
  106.3 51.6 %copy-start.61 = (f32[256]{0:T(256)S(1)}, f32[256]{0:T(256)}, u32[]{:S(2)}) copy-start(f32[256]{0:T(256)} %copy-done.60) | copy-start | bytes 3076
  106.3 51.6 %copy-start.63 = (f32[256]{0:T(256)S(1)}, f32[256]{0:T(256)}, u32[]{:S(2)}) copy-start(f32[256]{0:T(256)} %copy-done.62) | copy-start | bytes 3076
  106.3 155.4 %all-reduce.10.cloned.1.call-start = ((), (), s32[]{:S(2)}) async-start(), calls=%async_computation.18 | async-start | bytes 8388608 | tf_op jit(solution)/shard_map/psum | solution.py:94
  112.3 48.3 %copy-start.17 = (bf16[256,2048]{1,0:T(8,128)(2,1)S(1)}, bf16[256,2048]{1,0:T(8,128)(2,1)}, u32[]{:S(2)}) copy-start(bf16[256,2048]{1,0:T(8,128)(2,1)} %param.31) | copy-start | bytes 3145732
  112.3 48.3 %copy-start.65 = (f32[256]{0:T(256)S(1)}, f32[256]{0:T(256)}, u32[]{:S(2)}) copy-start(f32[256]{0:T(256)} %copy-done.64) | copy-start | bytes 3076
  165.2 6.3 copy-start.24
  175.9 179.3 %reduce-scatter.11.cloned.1.call-start = ((), (), s32[]{:S(2)}) async-start(), calls=%async_computation.11 | async-start | bytes 4718592 | tf_op jit(solution)/shard_map/reduce_scatter | solution.py:161
  180.0 267.2 %reduce-scatter.9.cloned.1.call-start = ((), (), s32[]{:S(2)}) async-start(), calls=%async_computation.10 | async-start | bytes 4718592 | tf_op jit(solution)/shard_map/reduce_scatter | solution.py:160
  183.9 396.7 %reduce-scatter.21.cloned.1.call-start = ((), (), s32[]{:S(2)}) async-start(), calls=%async_computation.16 | async-start | bytes 7962624 | tf_op jit(solution)/shard_map/reduce_scatter | solution.py:166
  189.7 523.9 %reduce-scatter.23.cloned.1.call-start = ((), (), s32[]{:S(2)}) async-start(), calls=%async_computation.17 | async-start | bytes 7962624 | tf_op jit(solution)/shard_map/reduce_scatter | solution.py:167
  196.0 650.6 %reduce-scatter.19.cloned.1.call-start = ((), (), s32[]{:S(2)}) async-start(), calls=%async_computation.15 | async-start | bytes 7962624 | tf_op jit(solution)/shard_map/reduce_scatter | solution.py:165
  201.4 778.2 %reduce-scatter.17.cloned.1.call-start = ((), (), s32[]{:S(2)}) async-start(), calls=%async_computation.14 | async-start | bytes 7962624 | tf_op jit(solution)/shard_map/reduce_scatter | solution.py:164
  207.3 905.2 %reduce-scatter.13.cloned.1.call-start = ((), (), s32[]{:S(2)}) async-start(), calls=%async_computation.12 | async-start | bytes 7962624 | tf_op jit(solution)/shard_map/reduce_scatter | solution.py:162
  212.5 1033.0 %reduce-scatter.15.cloned.1.call-start = ((), (), s32[]{:S(2)}) async-start(), calls=%async_computation.13 | async-start | bytes 7962624 | tf_op jit(solution)/shard_map/reduce_scatter | solution.py:163
  265.1 43.0 %copy-start.48 = (f32[256]{0:T(256)S(1)}, f32[256]{0:T(256)}, u32[]{:S(2)}) copy-start(f32[256]{0:T(256)} %copy-done.46) | copy-start | bytes 3076
  265.1 43.0 %copy-start.51 = (f32[256]{0:T(256)S(1)}, f32[256]{0:T(256)}, u32[]{:S(2)}) copy-start(f32[256]{0:T(256)} %copy-done.49) | copy-start | bytes 3076
  307.2 938.3 %copy-start.1 = (bf16[2048,864]{0,1:T(8,128)(2,1)S(1)}, bf16[2048,864]{0,1:T(8,128)(2,1)}, u32[]{:S(2)}) copy-start(bf16[2048,864]{0,1:T(8,128)(2,1)} %param.23) | copy-start | bytes 10616836
  (57 other events, 110.9 us)
Sparse Core Ops, SparseCore 0:
  40.3 54.0 all-reduce.5
  106.4 51.4 all-reduce.7
  176.0 85.5 all-reduce.9
  265.7 89.4 reduce-scatter.10
  359.2 87.9 reduce-scatter.8
  451.4 129.1 reduce-scatter.20
  584.9 128.6 reduce-scatter.22
  717.9 128.6 reduce-scatter.18
  850.9 128.6 reduce-scatter.16
  983.8 128.6 reduce-scatter.12
  1116.8 128.6 reduce-scatter.14
where the time goes:
time: 1250 us
  waiting for transfers between devices  1070 us (86%)
  matrix products  80.6 us (6%)
  blocking collectives  40.5 us (3%)
  other arithmetic  25.9 us (2%)
  local copies, waits for them, and re-layouts  18.7 us (1%)
  between operations  14.7 us (1%)
    reduce_scatter x1, waiting for transfers between devices, body(): lax.psum_scatter(grad_linear, 'dp', scatter_dimension=0, tiled=True)  133 us
    reduce_scatter x1, waiting for transfers between devices, body(): lax.psum_scatter(grad_out, 'dp', scatter_dimension=1, tiled=True)  133 us
    reduce_scatter x1, waiting for transfers between devices, body(): lax.psum_scatter(grad_gate, 'dp', scatter_dimension=0, tiled=True)  133 us
    reduce_scatter x1, waiting for transfers between devices, body(): lax.psum_scatter(grad_down, 'dp', scatter_dimension=1, tiled=True)  133 us
    reduce_scatter x1, waiting for transfers between devices, body(): lax.psum_scatter(grad_inner, 'dp', scatter_dimension=0, tiled=True)  133 us
    reduce_scatter x1, waiting for transfers between devices, body(): lax.psum_scatter(grad_value, 'dp', scatter_dimension=0, tiled=True)  133 us
    reduce_scatter x1, waiting for transfers between devices, body(): lax.psum_scatter(grad_query, 'dp', scatter_dimension=0, tiled=True)  92.1 us
    psum x1, waiting for transfers between devices, body(): lax.psum(jnp.dot(gated, out_weight, preferred_element_type=f32), 'tensor')  48.4 us
  transfers between devices with their start and end apart: 11, of which 11 were waited for; matrix products, arithmetic and copies ran while one was open for 5% of the time, Pallas kernels for 0%

commit v1 on v0

v1 whole, which is shorter than its diff:
```python
import jax
import jax.numpy as jnp
from jax import lax
from jax.sharding import PartitionSpec as P

KD = 256
VD = 432
DOCS_DEV = 8
GROUP = 4
PAIR = 2

EPS = 1e-05
HEAD_EPS = 0.25

F32 = jnp.float32
BF16 = jnp.bfloat16
AXES = ("dp", "tensor")


def dot(a, b, contract):
    return lax.dot_general(a, b, (contract, ((), ())), preferred_element_type=F32)


def nn(a, b):
    return dot(a, b, ((1,), (0,)))


def nt(a, b):
    return dot(a, b, ((1,), (1,)))


def tn(a, b):
    return dot(a, b, ((0,), (0,)))


def bdot(a, b, ca, cb):
    return lax.dot_general(a, b, (((ca,), (cb,)), ((0,), (0,))), preferred_element_type=F32)


def norm_rows(value, gain, bias, epsilon):
    center = value - jnp.mean(value, -1, keepdims=True)
    inverse = lax.rsqrt(jnp.mean(center * center, -1, keepdims=True) + epsilon)
    unit = center * inverse
    return (unit * gain + bias, unit, inverse)


def norm_back(upstream, unit, inverse, gain):
    scaled = upstream * gain
    return inverse * (
        scaled
        - jnp.mean(scaled, -1, keepdims=True)
        - unit * jnp.mean(scaled * unit, -1, keepdims=True)
    )


def decay_tables(document, first_head, head_count):
    rows = document.shape[1]
    places = jnp.arange(rows)
    spread = (places[:, None] - places[None, :]).astype(F32)
    allowed = (places[:, None] >= places[None, :])[None] & (
        document[:, :, None] == document[:, None, :]
    )
    safe = jnp.where(allowed, spread[None], 0.0)
    tables = []
    for h in range(head_count):
        log_rate = jnp.log1p(-jnp.exp2(-5.0 - (first_head + h).astype(F32)))
        tables.append(jnp.where(allowed, jnp.exp(safe * log_rate), 0.0))
    return tables


def head_mean(value, head_count):
    column = lax.broadcasted_iota(jnp.int32, (1, value.shape[1]), 1)
    out = None
    for h in range(head_count):
        mine = (column >= h * VD) & (column < (h + 1) * VD)
        mean = jnp.sum(jnp.where(mine, value, 0.0), -1, keepdims=True) * (1.0 / VD)
        out = mean if out is None else jnp.where(column >= h * VD, mean, out)
    return out


def by_head(parts):
    column = lax.broadcasted_iota(jnp.int32, (1, 1, parts[0].shape[-1]), 2)
    out = parts[0]
    for h in range(1, len(parts)):
        out = jnp.where(column >= h * VD, parts[h], out)
    return out


def head_only(value, h):
    column = lax.broadcasted_iota(jnp.int32, (1, value.shape[1]), 1)
    mine = (column >= h * VD) & (column < (h + 1) * VD)
    return jnp.where(mine, value, jnp.zeros((), value.dtype))


def retention_forward(normed, document, weights, head_gain, first_head):
    query_weight, key_weight, value_weight, gate_weight = weights
    blocks, rows = document.shape
    heads = query_weight.shape[1] // KD
    query = nn(normed, query_weight).astype(BF16)
    key = (nn(normed, key_weight) * KD ** (-0.5)).astype(BF16)
    value = nn(normed, value_weight).astype(BF16)
    gates = nn(normed, gate_weight)
    decay = decay_tables(document, first_head, heads)
    cube = lambda z: z.reshape(blocks, rows, z.shape[-1])
    value3 = cube(value)
    scores, parts, queries, keys = [], [], [], []
    for h in range(heads):
        queries.append(cube(query[:, h * KD : (h + 1) * KD]))
        keys.append(cube(key[:, h * KD : (h + 1) * KD]))
        scores.append((bdot(queries[h], keys[h], 2, 2) * decay[h]).astype(BF16))
        parts.append(bdot(scores[h], value3, 2, 1))
    mixed = by_head(parts).reshape(blocks * rows, value.shape[1])
    center = mixed - head_mean(mixed, heads)
    inverse = lax.rsqrt(head_mean(center * center, heads) + HEAD_EPS)
    hat = center * inverse
    normed_heads = hat * head_gain
    sigma = jax.nn.sigmoid(gates)
    swish = gates * sigma
    gated = (swish * normed_heads).astype(BF16)
    return gated, (queries, keys, value3, scores, decay, gates, hat, inverse)


def retention_backward(grad_middle_bf, state, out_weight, head_gain):
    queries, keys, value3, scores, decay, gates, hat, inverse = state
    heads = len(scores)
    blocks, rows, width = value3.shape
    grad_gated = nt(grad_middle_bf, out_weight)
    sigma = jax.nn.sigmoid(gates)
    swish = gates * sigma
    normed_heads = hat * head_gain
    grad_gates = (grad_gated * normed_heads * sigma * (1.0 + gates * (1.0 - sigma))).astype(BF16)
    grad_normed = grad_gated * swish
    scaled = grad_normed * head_gain
    grad_mixed = (
        inverse * (scaled - head_mean(scaled, heads) - hat * head_mean(scaled * hat, heads))
    ).astype(BF16)
    cube = lambda z: z.reshape(blocks, rows, z.shape[-1])
    flat = lambda z: z.reshape(blocks * rows, z.shape[-1])
    mixed3 = cube(grad_mixed)
    grad_query, grad_key, parts = [], [], []
    for h in range(heads):
        grad_scores = bdot(cube(head_only(grad_mixed, h)), value3, 2, 2)
        masked = (grad_scores * decay[h]).astype(BF16)
        grad_query.append(flat(bdot(masked, keys[h], 2, 1).astype(BF16)))
        grad_key.append(flat((bdot(masked, queries[h], 1, 1) * KD ** (-0.5)).astype(BF16)))
        parts.append(bdot(scores[h], mixed3, 1, 1))
    grad_value = flat(by_head(parts).astype(BF16))
    return (
        jnp.concatenate(grad_query, 1),
        jnp.concatenate(grad_key, 1),
        grad_value,
        grad_gates,
        grad_normed,
    )


def mlp(normed, grad_top_bf, inner_weight, linear_weight, down_weight):
    inner = nn(normed, inner_weight)
    linear = nn(normed, linear_weight)
    grad_hidden = nt(grad_top_bf, down_weight)
    cumulative = 0.5 * (1.0 + jax.scipy.special.erf(inner * 0.7071067811865476))
    gelu_inner = inner * cumulative
    hidden = (gelu_inner * linear).astype(BF16)
    slope = cumulative + inner * jnp.exp(-0.5 * inner * inner) * 0.3989422804014327
    grad_inner = (grad_hidden * linear * slope).astype(BF16)
    grad_linear = (grad_hidden * gelu_inner).astype(BF16)
    return hidden, grad_inner, grad_linear


def make_body(dp, tp):
    hi_count = dp // (GROUP * PAIR)

    def permute(x, target):
        pairs = []
        for d in range(dp):
            for t in range(tp):
                to_d, to_t = target(d, t)
                pairs.append((d * tp + t, to_d * tp + to_t))
        return lax.ppermute(x, AXES, pairs)

    swap_core = lambda x: permute(x, lambda d, t: (d, t ^ 1))
    swap_row = lambda x: permute(x, lambda d, t: (d, t ^ 2))
    swap_dp = lambda x, bit: permute(x, lambda d, t: (d ^ bit, t))

    def body(
        inputs,
        document,
        query_weight,
        key_weight,
        value_weight,
        gate_weight,
        out_weight,
        inner_weight,
        linear_weight,
        down_weight,
        first_gain,
        first_bias,
        head_gain,
        second_gain,
        second_bias,
        cotangent,
    ):
        rows, width = inputs.shape
        quarter = width // tp
        share = width // dp
        heads = query_weight.shape[1] // KD
        d = lax.axis_index("dp")
        t = lax.axis_index("tensor")
        core = t % 2
        row = t // 2
        low = d % PAIR
        first_head = t * heads
        projections = (query_weight, key_weight, value_weight, gate_weight)

        def joined(mine, other, place):
            return jnp.where(
                place == 0,
                jnp.concatenate([mine, other], 1),
                jnp.concatenate([other, mine], 1),
            )

        def halves(x, place):
            n = x.shape[1] // 2
            keep = lax.dynamic_slice_in_dim(x, place * n, n, 1)
            send = lax.dynamic_slice_in_dim(x, (1 - place) * n, n, 1)
            return keep, send

        def gather_columns(part):
            half = joined(part, swap_row(part), row)
            return joined(half, swap_core(half), core)

        def reduce_columns(x):
            keep, send = halves(x, core)
            x = keep + swap_core(send)
            keep, send = halves(x, row)
            return keep + swap_row(send)

        def my_columns(x):
            return lax.dynamic_slice_in_dim(x, (core * 2 + row) * quarter, quarter, 1)

        def others(part):
            blocks = [gather_columns(swap_dp(part, k * PAIR)) for k in range(1, GROUP)]
            return jnp.concatenate(blocks, 0)

        def shares(x, which):
            group = (d // PAIR) % GROUP
            cuts = [
                lax.dynamic_slice_in_dim(
                    x, ((hi * GROUP + group) * PAIR + which) * share, share, 1
                )
                for hi in range(hi_count)
            ]
            return cuts[0] if hi_count == 1 else jnp.concatenate(cuts, 1)

        def over_hi(x, axis):
            hi = d // (GROUP * PAIR)
            cut = lambda k: lax.dynamic_slice_in_dim(x, (hi ^ k) * share, share, axis)
            total = cut(0)
            for k in range(1, hi_count):
                total = total + swap_dp(cut(k), k * GROUP * PAIR)
            return total

        def summed(left, right, transposed):
            def product(which):
                a = shares(left, which)
                return tn(right, a) if transposed else tn(a, right)

            arrived = swap_dp(product(1 - low), 1)
            return over_hi(product(low) + arrived, 1 if transposed else 0)

        residual = inputs.astype(F32)
        cotangent_f = cotangent.astype(F32)
        other_inputs = others(my_columns(residual))
        other_document = jnp.stack([swap_dp(document, k * PAIR) for k in range(1, GROUP)])
        other_cotangent = others(my_columns(cotangent_f))

        first_norm, first_hat, first_inv = norm_rows(residual, first_gain, first_bias, EPS)
        normed_one = first_norm.astype(BF16)
        gated, state = retention_forward(
            normed_one, document[None], projections, head_gain, first_head
        )
        branch = reduce_columns(nn(gated, out_weight))
        middle_part = my_columns(residual) + branch
        middle = gather_columns(middle_part)
        other_middle = others(middle_part)

        second_norm, second_hat, second_inv = norm_rows(middle, second_gain, second_bias, EPS)
        normed_two = second_norm.astype(BF16)
        grad_top = cotangent_f * (document < DOCS_DEV).astype(F32)[:, None]
        grad_top_bf = grad_top.astype(BF16)
        hidden, grad_inner_bf, grad_linear_bf = mlp(
            normed_two, grad_top_bf, inner_weight, linear_weight, down_weight
        )
        upstream_two_part = reduce_columns(
            nt(grad_inner_bf, inner_weight) + nt(grad_linear_bf, linear_weight)
        )
        upstream_two = gather_columns(upstream_two_part)
        other_upstream_two = others(upstream_two_part)
        grad_middle = grad_top + norm_back(upstream_two, second_hat, second_inv, second_gain)
        grad_middle_bf = grad_middle.astype(BF16)
        grad_query_bf, grad_key_bf, grad_value_bf, grad_gates_bf, grad_normed = retention_backward(
            grad_middle_bf, state, out_weight, head_gain
        )
        upstream_one = gather_columns(
            reduce_columns(
                nt(grad_query_bf, query_weight)
                + nt(grad_key_bf, key_weight)
                + nt(grad_value_bf, value_weight)
                + nt(grad_gates_bf, gate_weight)
            )
        )
        grad_inputs = grad_middle + norm_back(upstream_one, first_hat, first_inv, first_gain)
        outputs = gather_columns(middle_part + reduce_columns(nn(hidden, down_weight)))

        other_normed_one = norm_rows(other_inputs, first_gain, first_bias, EPS)[0].astype(BF16)
        other_gated, other_state = retention_forward(
            other_normed_one, other_document, projections, head_gain, first_head
        )
        other_live = (other_document < DOCS_DEV).astype(F32).reshape(-1, 1)
        other_top = other_cotangent * other_live
        other_top_bf = other_top.astype(BF16)
        other_norm, other_hat, other_inv = norm_rows(other_middle, second_gain, second_bias, EPS)
        other_normed_two = other_norm.astype(BF16)
        other_hidden, other_inner_bf, other_linear_bf = mlp(
            other_normed_two, other_top_bf, inner_weight, linear_weight, down_weight
        )
        stack = lambda a, b: jnp.concatenate([a, b], 0)
        all_two = stack(normed_two, other_normed_two)
        all_top = stack(grad_top_bf, other_top_bf)
        grad_down = summed(all_top, stack(hidden, other_hidden), True)
        grad_inner = summed(all_two, stack(grad_inner_bf, other_inner_bf), False)
        grad_linear = summed(all_two, stack(grad_linear_bf, other_linear_bf), False)

        other_middle_bf = (
            other_top + norm_back(other_upstream_two, other_hat, other_inv, second_gain)
        ).astype(BF16)
        other_query_bf, other_key_bf, other_value_bf, other_gates_bf, unused = retention_backward(
            other_middle_bf, other_state, out_weight, head_gain
        )
        all_one = stack(normed_one, other_normed_one)
        grad_out = summed(
            stack(grad_middle_bf, other_middle_bf), stack(gated, other_gated), True
        )
        grad_gate = summed(all_one, stack(grad_gates_bf, other_gates_bf), False)
        grad_value = summed(all_one, stack(grad_value_bf, other_value_bf), False)
        grad_query = summed(all_one, stack(grad_query_bf, other_query_bf), False)
        grad_key = summed(all_one, stack(grad_key_bf, other_key_bf), False)

        sums = [
            jnp.sum(upstream_two * second_hat, 0),
            jnp.sum(upstream_two, 0),
            jnp.sum(grad_normed * state[6], 0),
            jnp.sum(upstream_one * first_hat, 0),
            jnp.sum(upstream_one, 0),
        ]
        total = jnp.concatenate(sums)
        bit = 1
        while bit < dp:
            total = total + swap_dp(total, bit)
            bit *= 2
        ends = []
        at = 0
        for s in sums:
            ends.append(total[at : at + s.shape[0]])
            at += s.shape[0]
        second_gain_sum, second_bias_sum, head_gain_sum, first_gain_sum, first_bias_sum = ends
        return (
            outputs,
            grad_inputs,
            grad_query,
            grad_key,
            grad_value,
            grad_gate,
            grad_out,
            grad_inner,
            grad_linear,
            grad_down,
            first_gain_sum,
            first_bias_sum,
            head_gain_sum,
            second_gain_sum,
            second_bias_sum,
        )

    return body


def solution(mesh):
    in_specs = (
        P("dp", None),
        P("dp"),
        P(None, "tensor"),
        P(None, "tensor"),
        P(None, "tensor"),
        P(None, "tensor"),
        P("tensor", None),
        P(None, "tensor"),
        P(None, "tensor"),
        P("tensor", None),
        P(),
        P(),
        P("tensor"),
        P(),
        P(),
        P("dp", None),
    )
    out_specs = (
        P("dp", None),
        P("dp", None),
        P("dp", "tensor"),
        P("dp", "tensor"),
        P("dp", "tensor"),
        P("dp", "tensor"),
        P("tensor", "dp"),
        P("dp", "tensor"),
        P("dp", "tensor"),
        P("tensor", "dp"),
        P(),
        P(),
        P("tensor"),
        P(),
        P(),
    )
    body = make_body(mesh.shape["dp"], mesh.shape["tensor"])
    return jax.shard_map(body, mesh=mesh, in_specs=in_specs, out_specs=out_specs, check_vma=False)
```

time: 1250 us -> 678 us (0.54)
  waiting for transfers between devices: 1070 us -> 278 us
  other arithmetic: 25.9 us -> 145 us
  starting transfers between devices: 1.12 us -> 74 us
  local copies, waits for them, and re-layouts: 18.7 us -> 59.4 us
  blocking collectives: 40.5 us -> 0 us
  matrix products: 80.6 us -> 113 us
    reduce_scatter x8 -> x0, waiting for transfers between devices: 933 us -> none  [the longest x1 133 us: body(): lax.psum_scatter(grad_linear, 'dp', scatter_dimension=0, tiled=True)]
    ppermute x0 -> x66, waiting for transfers between devices: none -> 278 us  [permute(): return lax.ppermute(x, AXES, pairs)]
    psum x3 -> x0, waiting for transfers between devices: 138 us -> none  [the longest x1 48.4 us: body(): lax.psum(jnp.dot(gated, out_weight, preferred_element_type=f32), 'tensor')]
    ppermute x0 -> x66, starting transfers between devices: none -> 74 us  [permute(): return lax.ppermute(x, AXES, pairs)]
    select_n x1 -> x31, other arithmetic: 1.67 us -> 65 us  [the longest x29 56.4 us: joined(): jnp.where(place == 0, jnp.concatenate([mine, other], 1), jnp.concatenate(...]
    psum x1 -> x0, blocking collectives: 40.5 us -> none  [body(): lax.psum((grad_first_gain, grad_first_bias, grad_gain_heads.reshape(local...]
    dot_general x30 -> x64, matrix products: 80.6 us -> 113 us  [the longest x40 88.4 us: dot(): lax.dot_general(a, b, (contract, ((), ())), preferred_element_type=F32)]
    convert_element_type x3 -> x13, other arithmetic: 1.39 us -> 28.9 us  [the longest x1 8.94 us: body(): other_normed_two = other_norm.astype(BF16)]
  transfers between devices with their start and end apart: 11 -> 66, of which waited for: 11 -> 28; matrix products, arithmetic and copies ran while one was open for 5% -> 40% of each run, Pallas kernels for 0% -> 0%
where the time goes in v1:
time: 678 us; the launch traced here: 673 us
  waiting for transfers between devices  278 us (41%)
  other arithmetic  145 us (21%)
  matrix products  113 us (17%)
  starting transfers between devices  74 us (11%)
  local copies, waits for them, and re-layouts  59.4 us (9%)
    ppermute x66, waiting for transfers between devices, permute(): return lax.ppermute(x, AXES, pairs)  278 us
    dot_general x40, matrix products, dot(): lax.dot_general(a, b, (contract, ((), ())), preferred_element_type=F32)  88.4 us
    ppermute x66, starting transfers between devices, permute(): return lax.ppermute(x, AXES, pairs)  74 us
    select_n x29, other arithmetic, joined(): jnp.where(place == 0, jnp.concatenate([mine, other], 1), jnp.concatenate(...  56.4 us
    dot_general x24, matrix products, bdot(): lax.dot_general(a, b, (((ca,), (cb,)), ((0,), (0,))), preferred_element_t...  24.8 us
    unnamed x362, local copies, waits for them, and re-layouts  16.1 us
  transfers between devices with their start and end apart: 66, of which 28 were waited for; matrix products, arithmetic and copies ran while one was open for 40% of the time, Pallas kernels for 0%

profile of v1, /device:TPU:0, one launch (start us, length us, event | category | flops | bytes accessed | tf_op | source)
XLA Modules:
  0.0 672.6 jit_solution(11334512915337559691)
XLA Ops:
  48.1 15.1 %collective-permute-done.28 = f32[256,512]{1,0:T(8,128)} collective-permute-done((f32[256,512]{1,0:T(8,128)}, f32[256,512]{1,0:T(8,128)}, u32[]{:S(2)}, u32[]{:S(2)}) %collective-permute-start.28) | collective-permute-done | bytes 524320 | tf_op jit(solution)/shard_map/ppermute | solution.py:179
  64.9 13.1 %collective-permute-done.31 = f32[256,512]{1,0:T(8,128)} collective-permute-done((f32[256,512]{1,0:T(8,128)}, f32[256,512]{1,0:T(8,128)}, u32[]{:S(2)}, u32[]{:S(2)}) %collective-permute-start.31) | collective-permute-done | bytes 524320 | tf_op jit(solution)/shard_map/ppermute | solution.py:179
  87.6 5.4 collective-permute-done.32
  95.4 8.9 %collective-permute-done.1 = f32[256,512]{1,0:T(8,128)S(1)} collective-permute-done((f32[256,512]{1,0:T(8,128)S(1)}, f32[256,512]{1,0:T(8,128)S(1)}, u32[]{:S(2)}, u32[]{:S(2)}) %collective-permute-start.1) | collective-permute-done | bytes 524320 | tf_op jit(solution)/shard_map/ppermute | solution.py:179
  107.9 7.6 %collective-permute-done.35 = f32[256,512]{1,0:T(8,128)S(1)} collective-permute-done((f32[256,512]{1,0:T(8,128)}, f32[256,512]{1,0:T(8,128)S(1)}, u32[]{:S(2)}, u32[]{:S(2)}) %collective-permute-start.35) | collective-permute-done | bytes 524320 | tf_op jit(solution)/shard_map/ppermute | solution.py:179
  148.8 7.3 %collective-permute-done.37 = f32[256,512]{1,0:T(8,128)S(1)} collective-permute-done((f32[256,512]{1,0:T(8,128)}, f32[256,512]{1,0:T(8,128)S(1)}, u32[]{:S(2)}, u32[]{:S(2)}) %collective-permute-start.37) | collective-permute-done | bytes 524320 | tf_op jit(solution)/shard_map/ppermute | solution.py:179
  159.1 10.9 %collective-permute-done.40 = f32[256,512]{1,0:T(8,128)S(1)} collective-permute-done((f32[256,512]{1,0:T(8,128)}, f32[256,512]{1,0:T(8,128)S(1)}, u32[]{:S(2)}, u32[]{:S(2)}) %collective-permute-start.40) | collective-permute-done | bytes 524320 | tf_op jit(solution)/shard_map/ppermute | solution.py:179
  171.6 6.5 collective-permute-done.16
  179.6 35.4 %collective-permute-done.19 = f32[256,512]{1,0:T(8,128)S(1)} collective-permute-done((f32[256,512]{1,0:T(8,128)S(1)}, f32[256,512]{1,0:T(8,128)S(1)}, u32[]{:S(2)}, u32[]{:S(2)}) %collective-permute-start.19) | collective-permute-done | bytes 524320 | tf_op jit(solution)/shard_map/ppermute | solution.py:179
  231.0 10.0 %collective-permute-done.17 = f32[256,512]{1,0:T(8,128)S(1)} collective-permute-done((f32[256,512]{1,0:T(8,128)S(1)}, f32[256,512]{1,0:T(8,128)S(1)}, u32[]{:S(2)}, u32[]{:S(2)}) %collective-permute-start.17) | collective-permute-done | bytes 524320 | tf_op jit(solution)/shard_map/ppermute | solution.py:179
  241.2 10.7 %collective-permute-done.20 = f32[256,512]{1,0:T(8,128)S(1)} collective-permute-done((f32[256,512]{1,0:T(8,128)S(1)}, f32[256,512]{1,0:T(8,128)S(1)}, u32[]{:S(2)}, u32[]{:S(2)}) %collective-permute-start.20) | collective-permute-done | bytes 524320 | tf_op jit(solution)/shard_map/ppermute | solution.py:179
  252.1 5.4 collective-permute-done.23
  318.4 11.3 %collective-permute-done.9 = f32[256,512]{1,0:T(8,128)S(1)} collective-permute-done((f32[256,512]{1,0:T(8,128)S(1)}, f32[256,512]{1,0:T(8,128)S(1)}, u32[]{:S(2)}, u32[]{:S(2)}) %collective-permute-start.9) | collective-permute-done | bytes 524320 | tf_op jit(solution)/shard_map/ppermute | solution.py:179
  333.0 6.6 collective-permute-start.46
  345.1 7.0 %collective-permute-done.10 = f32[256,512]{1,0:T(8,128)S(1)} collective-permute-done((f32[256,512]{1,0:T(8,128)}, f32[256,512]{1,0:T(8,128)S(1)}, u32[]{:S(2)}, u32[]{:S(2)}) %collective-permute-start.10) | collective-permute-done | bytes 524320 | tf_op jit(solution)/shard_map/ppermute | solution.py:179
  354.5 6.0 collective-permute-done.46
  456.5 8.9 %add_convert_fusion = (bf16[768,2048]{1,0:T(8,128)(2,1)}, bf16[768,2048]{1,0:T(8,128)(2,1)}) fusion(f32[2048]{0:T(1024)S(1)} %copy-done.134, f32[2048]{0:T(1024)S(1)} %copy-done.116, f32[768]{0:T(1024)S(1)} %copy-done.132, f32[768]{0:T(1024)S(1)} %copy-done.125, f32[256,2048]{1,0:T(8,128)} %copy-done.8, f32[256,2048]{1,0:T(8,128)} %copy-done.6, ...), kind=kLoop, calls=%fused_computation.4 | loop fusion | flops 29884416 | bytes 25197568 | tf_op jit(solution)/shard_map/convert_element_type | solution.py:323
  465.5 9.4 %select_reduce_fusion.1 = (f32[768]{0:T(1024)S(1)}, f32[768]{0:T(1024)S(1)}, f32[768]{0:T(1024)S(1)}, f32[768]{0:T(1024)S(1)}, f32[768,864]{0,1:T(8,128)S(1)}, /...) fusion(pred[864]{0:T(1024)(128)(4,1)S(1)} %copy-done.140, f32[768]{0:T(1024)S(1)} %copy-done.155, ...), kind=kOutput, calls=%fused_computation.47 | convolution fusion | flops 2737812480 | bytes 17332128 | tf_op jit(solution)/shard_map/dot_general | solution.py:21
  474.9 6.1 broadcast_select_fusion.1
  532.6 26.0 %collective-permute-done.56 = f32[256,512]{1,0:T(8,128)S(1)} collective-permute-done((f32[256,512]{1,0:T(8,128)S(1)}, f32[256,512]{1,0:T(8,128)S(1)}, u32[]{:S(2)}, u32[]{:S(2)}) %collective-permute-start.56) | collective-permute-done | bytes 524320 | tf_op jit(solution)/shard_map/ppermute | solution.py:179
  561.3 8.5 %collective-permute-done.55 = f32[256,512]{1,0:T(8,128)S(1)} collective-permute-done((f32[256,512]{1,0:T(8,128)S(1)}, f32[256,512]{1,0:T(8,128)S(1)}, u32[]{:S(2)}, u32[]{:S(2)}) %collective-permute-start.55) | collective-permute-done | bytes 524320 | tf_op jit(solution)/shard_map/ppermute | solution.py:179
  585.1 41.6 %collective-permute-done.57 = f32[256,864]{0,1:T(8,128)S(1)} collective-permute-done((f32[256,864]{0,1:T(8,128)S(1)}, f32[256,864]{0,1:T(8,128)S(1)}, u32[]{:S(2)}, u32[]{:S(2)}) %collective-permute-start.57) | collective-permute-done | bytes 884768 | tf_op jit(solution)/shard_map/ppermute | solution.py:179
  631.6 13.2 %collective-permute-done.58 = f32[256,864]{0,1:T(8,128)S(1)} collective-permute-done((f32[256,864]{0,1:T(8,128)S(1)}, f32[256,864]{0,1:T(8,128)S(1)}, u32[]{:S(2)}, u32[]{:S(2)}) %collective-permute-start.58) | collective-permute-done | bytes 884768 | tf_op jit(solution)/shard_map/ppermute | solution.py:179
  654.4 6.3 collective-permute-start.64
  (670 shorter events, 381.8 us)
Async XLA Ops:
  31.8 47.8 %collective-permute-start = (f32[256,1024]{1,0:T(8,128)}, f32[256,1024]{1,0:T(8,128)}, u32[]{:S(2)}, u32[]{:S(2)}) collective-permute-start(f32[256,1024]{1,0:T(8,128)} %constant_dynamic-slice_fusion.8), channel_id=1, source_target_pairs={{0,1},{1,0},{2,3},{3,2},{4,5},{5,4},{6,7},{7,6},{8,9},{9,8},{10,11... | collective-permute-start | bytes 3145736 | tf_op jit(solution)/shard_map/ppermute | solution.py:179
  42.1 77.2 %collective-permute-start.25 = (s32[256]{0:T(256)}, s32[256]{0:T(256)S(1)}, u32[]{:S(2)}, u32[]{:S(2)}) collective-permute-start(s32[256]{0:T(256)} %param.17), channel_id=1, source_target_pairs={{0,8},{1,9},{2,10},{3,11},{4,12},{5,13},{6,14},{7,15},{8,0},{9,1},... | collective-permute-start | bytes 3080 | tf_op jit(solution)/shard_map/ppermute | solution.py:179
  87.6 48.8 %collective-permute-start.30 = (f32[256,1024]{1,0:T(8,128)}, f32[256,1024]{1,0:T(8,128)}, u32[]{:S(2)}, u32[]{:S(2)}) collective-permute-start(f32[256,1024]{1,0:T(8,128)} %maximum_select_fusion.23), channel_id=1, source_target_pairs={{0,1},{1,0},{2,3},{3,2},{4,5},{5,4},{6,7},{7,6},{8,9},{9,8},{10,11... | collective-permute-start | bytes 3145736 | tf_op jit(solution)/shard_map/ppermute | solution.py:179
  95.4 45.1 %collective-permute-start.33 = (f32[256,1024]{1,0:T(8,128)}, f32[256,1024]{1,0:T(8,128)}, u32[]{:S(2)}, u32[]{:S(2)}) collective-permute-start(f32[256,1024]{1,0:T(8,128)} %maximum_select_fusion.24), channel_id=1, source_target_pairs={{0,1},{1,0},{2,3},{3,2},{4,5},{5,4},{6,7},{7,6},{8,9},{9,8},{10,11... | collective-permute-start | bytes 3145736 | tf_op jit(solution)/shard_map/ppermute | solution.py:179
  143.7 71.3 %collective-permute-start.19 = (f32[256,512]{1,0:T(8,128)S(1)}, f32[256,512]{1,0:T(8,128)S(1)}, u32[]{:S(2)}, u32[]{:S(2)}) collective-permute-start(f32[256,512]{1,0:T(8,128)S(1)} %copy-done.96), channel_id=1, source_target_pairs={{0,16},{1,17},{2,18},{3,19},{4,20},{5,21},{6,22},{7,23},{8,24},{9,... | collective-permute-start | bytes 1572872 | tf_op jit(solution)/shard_map/ppermute | solution.py:179
  156.1 60.5 %collective-permute-start.22 = (f32[256,512]{1,0:T(8,128)S(1)}, f32[256,512]{1,0:T(8,128)S(1)}, u32[]{:S(2)}, u32[]{:S(2)}) collective-permute-start(f32[256,512]{1,0:T(8,128)S(1)} %copy-done.96), channel_id=1, source_target_pairs={{0,24},{1,25},{2,26},{3,27},{4,28},{5,29},{6,30},{7,31},{8,16},{9,... | collective-permute-start | bytes 1572872 | tf_op jit(solution)/shard_map/ppermute | solution.py:179
  170.0 87.7 %collective-permute-start.3 = (f32[256,1024]{1,0:T(8,128)S(1)}, f32[256,1024]{1,0:T(8,128)S(1)}, u32[]{:S(2)}, u32[]{:S(2)}) collective-permute-start(f32[256,1024]{1,0:T(8,128)S(1)} %maximum_select_fusion.16), channel_id=1, source_target_pairs={{0,1},{1,0},{2,3},{3,2},{4,5},{5,4},{6,7},{7,6},{8,9},{9,8},{10,11... | collective-permute-start | bytes 3145736 | tf_op jit(solution)/shard_map/ppermute | solution.py:179
  170.1 51.4 %collective-permute-start.38 = (f32[256,512]{1,0:T(8,128)S(1)}, f32[256,512]{1,0:T(8,128)S(1)}, u32[]{:S(2)}, u32[]{:S(2)}) collective-permute-start(f32[256,512]{1,0:T(8,128)S(1)} %collective-permute-done.37), channel_id=1, source_target_pairs={{0,2},{1,3},{2,0},{3,1},{4,6},{5,7},{6,4},{7,5},{8,10},{9,11},{10,... | collective-permute-start | bytes 1572872 | tf_op jit(solution)/shard_map/ppermute | solution.py:179
  178.1 46.1 %collective-permute-start.41 = (f32[256,512]{1,0:T(8,128)S(1)}, f32[256,512]{1,0:T(8,128)S(1)}, u32[]{:S(2)}, u32[]{:S(2)}) collective-permute-start(f32[256,512]{1,0:T(8,128)S(1)} %collective-permute-done.40), channel_id=1, source_target_pairs={{0,2},{1,3},{2,0},{3,1},{4,6},{5,7},{6,4},{7,5},{8,10},{9,11},{10,... | collective-permute-start | bytes 1572872 | tf_op jit(solution)/shard_map/ppermute | solution.py:179
  229.8 63.3 %collective-permute-start.39 = (f32[256,1024]{1,0:T(8,128)}, f32[256,1024]{1,0:T(8,128)}, u32[]{:S(2)}, u32[]{:S(2)}) collective-permute-start(f32[256,1024]{1,0:T(8,128)} %maximum_select_fusion.26), channel_id=1, source_target_pairs={{0,1},{1,0},{2,3},{3,2},{4,5},{5,4},{6,7},{7,6},{8,9},{9,8},{10,11... | collective-permute-start | bytes 3145736 | tf_op jit(solution)/shard_map/ppermute | solution.py:179
  241.0 56.5 %collective-permute-start.42 = (f32[256,1024]{1,0:T(8,128)}, f32[256,1024]{1,0:T(8,128)}, u32[]{:S(2)}, u32[]{:S(2)}) collective-permute-start(f32[256,1024]{1,0:T(8,128)} %maximum_select_fusion.27), channel_id=1, source_target_pairs={{0,1},{1,0},{2,3},{3,2},{4,5},{5,4},{6,7},{7,6},{8,9},{9,8},{10,11... | collective-permute-start | bytes 3145736 | tf_op jit(solution)/shard_map/ppermute | solution.py:179
  354.5 44.7 %collective-permute-start.11 = (f32[256,1024]{1,0:T(8,128)}, f32[256,1024]{1,0:T(8,128)}, u32[]{:S(2)}, u32[]{:S(2)}) collective-permute-start(f32[256,1024]{1,0:T(8,128)} %maximum_select_fusion.18), channel_id=1, source_target_pairs={{0,1},{1,0},{2,3},{3,2},{4,5},{5,4},{6,7},{7,6},{8,9},{9,8},{10,11... | collective-permute-start | bytes 3145736 | tf_op jit(solution)/shard_map/ppermute | solution.py:179
  389.3 52.5 %collective-permute-start.48 = (f32[256,1024]{1,0:T(8,128)}, f32[256,1024]{1,0:T(8,128)}, u32[]{:S(2)}, u32[]{:S(2)}) collective-permute-start(f32[256,1024]{1,0:T(8,128)} %maximum_select_fusion.29), channel_id=1, source_target_pairs={{0,1},{1,0},{2,3},{3,2},{4,5},{5,4},{6,7},{7,6},{8,9},{9,8},{10,11... | collective-permute-start | bytes 3145736 | tf_op jit(solution)/shard_map/ppermute | solution.py:179
  393.6 50.9 %collective-permute-start.51 = (f32[256,1024]{1,0:T(8,128)}, f32[256,1024]{1,0:T(8,128)}, u32[]{:S(2)}, u32[]{:S(2)}) collective-permute-start(f32[256,1024]{1,0:T(8,128)} %maximum_select_fusion.30), channel_id=1, source_target_pairs={{0,1},{1,0},{2,3},{3,2},{4,5},{5,4},{6,7},{7,6},{8,9},{9,8},{10,11... | collective-permute-start | bytes 3145736 | tf_op jit(solution)/shard_map/ppermute | solution.py:179
  399.2 48.6 %collective-permute-start.54 = (f32[256,1024]{1,0:T(8,128)}, f32[256,1024]{1,0:T(8,128)}, u32[]{:S(2)}, u32[]{:S(2)}) collective-permute-start(f32[256,1024]{1,0:T(8,128)} %maximum_select_fusion.31), channel_id=1, source_target_pairs={{0,1},{1,0},{2,3},{3,2},{4,5},{5,4},{6,7},{7,6},{8,9},{9,8},{10,11... | collective-permute-start | bytes 3145736 | tf_op jit(solution)/shard_map/ppermute | solution.py:179
  427.6 100.0 %collective-permute-start.12 = (f32[256,1024]{1,0:T(8,128)}, f32[256,1024]{1,0:T(8,128)}, u32[]{:S(2)}, u32[]{:S(2)}) collective-permute-start(f32[256,1024]{1,0:T(8,128)} %constant_dynamic-slice_fusion.2), channel_id=1, source_target_pairs={{0,1},{1,0},{2,3},{3,2},{4,5},{5,4},{6,7},{7,6},{8,9},{9,8},{10,11... | collective-permute-start | bytes 3145736 | tf_op jit(solution)/shard_map/ppermute | solution.py:179
  505.7 67.6 %collective-permute-start.62 = (f32[864,256]{1,0:T(8,128)}, f32[864,256]{1,0:T(8,128)}, u32[]{:S(2)}, u32[]{:S(2)}) collective-permute-start(f32[864,256]{1,0:T(8,128)} %fusion.27), channel_id=1, source_target_pairs={{0,4},{1,5},{2,6},{3,7},{4,0},{5,1},{6,2},{7,3},{8,12},{9,13},{10,... | collective-permute-start | bytes 2654216 | tf_op jit(solution)/shard_map/ppermute | solution.py:179
  508.7 68.8 %collective-permute-start.61 = (f32[256,864]{0,1:T(8,128)}, f32[256,864]{0,1:T(8,128)}, u32[]{:S(2)}, u32[]{:S(2)}) collective-permute-start(f32[256,864]{0,1:T(8,128)} %fusion.28), channel_id=1, source_target_pairs={{0,4},{1,5},{2,6},{3,7},{4,0},{5,1},{6,2},{7,3},{8,12},{9,13},{10,... | collective-permute-start | bytes 2654216 | tf_op jit(solution)/shard_map/ppermute | solution.py:179
  522.8 47.0 %collective-permute-start.55 = (f32[256,512]{1,0:T(8,128)S(1)}, f32[256,512]{1,0:T(8,128)S(1)}, u32[]{:S(2)}, u32[]{:S(2)}) collective-permute-start(f32[256,512]{1,0:T(8,128)S(1)} %fusion.61), channel_id=1, source_target_pairs={{0,4},{1,5},{2,6},{3,7},{4,0},{5,1},{6,2},{7,3},{8,12},{9,13},{10,... | collective-permute-start | bytes 1572872 | tf_op jit(solution)/shard_map/ppermute | solution.py:179
  558.6 69.9 %collective-permute-start.60 = (f32[256,864]{0,1:T(8,128)S(1)}, f32[256,864]{0,1:T(8,128)S(1)}, u32[]{:S(2)}, u32[]{:S(2)}) collective-permute-start(f32[256,864]{0,1:T(8,128)S(1)} %fusion.29), channel_id=1, source_target_pairs={{0,4},{1,5},{2,6},{3,7},{4,0},{5,1},{6,2},{7,3},{8,12},{9,13},{10,... | collective-permute-start | bytes 2654216 | tf_op jit(solution)/shard_map/ppermute | solution.py:179
  569.8 60.2 %collective-permute-start.59 = (f32[864,256]{1,0:T(8,128)S(1)}, f32[864,256]{1,0:T(8,128)S(1)}, u32[]{:S(2)}, u32[]{:S(2)}) collective-permute-start(f32[864,256]{1,0:T(8,128)S(1)} %fusion.30), channel_id=1, source_target_pairs={{0,4},{1,5},{2,6},{3,7},{4,0},{5,1},{6,2},{7,3},{8,12},{9,13},{10,... | collective-permute-start | bytes 2654216 | tf_op jit(solution)/shard_map/ppermute | solution.py:179
  572.5 54.2 %collective-permute-start.57 = (f32[256,864]{0,1:T(8,128)S(1)}, f32[256,864]{0,1:T(8,128)S(1)}, u32[]{:S(2)}, u32[]{:S(2)}) collective-permute-start(f32[256,864]{0,1:T(8,128)S(1)} %fusion.20), channel_id=1, source_target_pairs={{0,4},{1,5},{2,6},{3,7},{4,0},{5,1},{6,2},{7,3},{8,12},{9,13},{10,... | collective-permute-start | bytes 2654216 | tf_op jit(solution)/shard_map/ppermute | solution.py:179
  577.5 67.2 %collective-permute-start.58 = (f32[256,864]{0,1:T(8,128)S(1)}, f32[256,864]{0,1:T(8,128)S(1)}, u32[]{:S(2)}, u32[]{:S(2)}) collective-permute-start(f32[256,864]{0,1:T(8,128)S(1)} %fusion.31), channel_id=1, source_target_pairs={{0,4},{1,5},{2,6},{3,7},{4,0},{5,1},{6,2},{7,3},{8,12},{9,13},{10,... | collective-permute-start | bytes 2654216 | tf_op jit(solution)/shard_map/ppermute | solution.py:179
  585.0 61.3 %collective-permute-start.15 = (f32[256,1024]{1,0:T(8,128)S(1)}, f32[256,1024]{1,0:T(8,128)S(1)}, u32[]{:S(2)}, u32[]{:S(2)}) collective-permute-start(f32[256,1024]{1,0:T(8,128)S(1)} %maximum_select_fusion.19), channel_id=1, source_target_pairs={{0,1},{1,0},{2,3},{3,2},{4,5},{5,4},{6,7},{7,6},{8,9},{9,8},{10,11... | collective-permute-start | bytes 3145736 | tf_op jit(solution)/shard_map/ppermute | solution.py:179
  (223 other events, 2456.9 us)
